TPU v7x, 32 devices: a whole 2x2x4 slice. The times are simulated.
32 devices in a mesh: expert: 4 (over y, core), dp: 8 (over z, x).
Axes of the slice: x: 2, y: 2, z: 4, core: 2. Of those that a mesh axis runs over, the one named last changes fastest.
Arguments:
- tokens: bfloat16 [32768, 2048], P(('expert', 'dp')), may hold values from -6 to 6
- block_expert: int32 [256, 1], P(('expert', 'dp')), may hold values from 0 to 3; in each aligned block of 8 rows (0 to 7, 8 to 15, ...) at most 4 rows name the same one
- gate_weight: bfloat16 [4, 2048, 768], P('expert', 'dp'), may hold values from -0.125 to 0.125
- up_weight: bfloat16 [4, 2048, 768], P('expert', 'dp'), may hold values from -0.125 to 0.125
- down_weight: bfloat16 [4, 768, 2048], P('expert', None, 'dp'), may hold values from -0.21875 to 0.21875
Outputs:
- r_factor: float32 [4, 768, 768], P('expert', 'dp')
- compressed_down: float32 [4, 768, 2048], P('expert', None, 'dp')
Inputs may be any that keep to these rules, and one draw needn't show every extreme that they name: `block_expert`: among the 8 blocks of one device, at most 4 name the same expert, and in every draw some device has exactly 4 blocks for one expert.
All inputs are finite; a program needn't handle non-finite values.
Results may differ from a plain program's by a relative error of at most 0.0003.
Values may be sent and summed in bfloat16 or wider, within the bound.
No kernel may reach another device: no remote copies, remote signals or barrier semaphores. Data moves between devices by JAX's collectives and lax.ppermute only.
A program may use at most 128 MiB of HBM per device.

v0:
```python
import jax
import jax.numpy as jnp
from jax import lax
from jax.sharding import PartitionSpec as P

BROWS = 128
damping = 0.05


def on_device(tokens, block_expert, gate_weight, up_weight, down_weight):
    n_expert = lax.axis_size("expert")
    n_data = lax.axis_size("dp")
    exp_local = gate_weight.shape[0]
    width = gate_weight.shape[2]
    model = tokens.shape[1]
    experts = exp_local * n_expert
    blk_count = block_expert.shape[0]
    capacity = max(2, 2 * blk_count // experts)
    rows_avg = blk_count * BROWS * n_data * n_expert // experts
    blocks = tokens.reshape(blk_count, BROWS, model)
    ids = block_expert[:, 0]
    positions = jnp.arange(blk_count, dtype=jnp.int32)
    same = ids[:, None] == ids[None, :]
    earlier = positions[None, :] < positions[:, None]
    ranks = jnp.sum((same & earlier).astype(jnp.int32), axis=1)
    slots = jnp.arange(experts * capacity, dtype=jnp.int32)
    match = (ids[None, :] == (slots // capacity)[:, None]) & (
        ranks[None, :] == (slots % capacity)[:, None]
    )
    found = jnp.sum(match.astype(jnp.int32), axis=1)
    source = jnp.sum(match.astype(jnp.int32) * positions[None, :], axis=1) + (1 - found) * blk_count
    padded = jnp.concatenate([blocks, jnp.zeros((1, BROWS, model), jnp.bfloat16)], axis=0)
    outgoing = padded[source].reshape(n_expert, exp_local, capacity, BROWS, model)
    arrived = lax.all_to_all(outgoing, "expert", split_axis=0, concat_axis=0, tiled=True)
    eye = jnp.eye(width, dtype=jnp.float32)
    my_rows = width // n_data
    rows = arrived[:, 0].reshape(-1, model)
    gate = jnp.dot(
        rows,
        lax.all_gather(gate_weight[0], "dp", axis=0, tiled=True),
        preferred_element_type=jnp.float32,
    )
    lifted = jnp.dot(
        rows,
        lax.all_gather(up_weight[0], "dp", axis=0, tiled=True),
        preferred_element_type=jnp.float32,
    )
    hidden = jax.nn.silu(gate) * lifted
    gram = jnp.dot(hidden.T, hidden, precision=lax.Precision.HIGHEST) / float(rows_avg)
    total = lax.psum(gram, "dp") + damping * eye
    upper = jnp.linalg.cholesky(total).T
    factors = [lax.dynamic_slice_in_dim(upper, lax.axis_index("dp") * my_rows, my_rows, 0)]
    products = [jnp.dot(upper, down_weight[0].astype(jnp.float32), precision=lax.Precision.HIGHEST)]
    return (jnp.stack(factors), jnp.stack(products))


def solution(mesh):
    placed = (
        P(("expert", "dp"), None),
        P(("expert", "dp"), None),
        P("expert", "dp", None),
        P("expert", "dp", None),
        P("expert", None, "dp"),
    )
    return jax.shard_map(
        on_device,
        mesh=mesh,
        in_specs=placed,
        out_specs=(P("expert", "dp", None), P("expert", None, "dp")),
        check_vma=False,
    )
```

profile of v0, /device:TPU:0, one launch (start us, length us, event | category | flops | bytes accessed | tf_op | source)
XLA Modules:
  0.0 432.7 jit_solution(1642863032886914557)
XLA Ops:
  7.2 0.0 copy-start
  7.2 0.0 all-gather.7.cloned.1.call-start
  7.2 0.7 all-gather.7.cloned.1.call-update
  7.9 0.0 copy-start.3
  7.9 5.0 %concatenate.3 = bf16[9,128,2048]{2,1,0:T(8,128)(2,1)} pad(bf16[8,128,2048]{2,1,0:T(8,128)(2,1)} %bitcast.59, bf16[]{:T(256)} %constant.236.clone.1), padding=0_1x0_0x0_0 | pad | bytes 8912898 | tf_op jit(solution)/shard_map/concatenate | solution.py:32
  12.9 0.0 copy-done.3
  12.9 0.2 convert_reduce_fusion.1
  13.1 0.1 convert_reduce_fusion
  13.2 7.1 %gather_fusion = bf16[16,128,2048]{2,1,0:T(8,128)(2,1)} fusion(bf16[9,128,2048]{2,1,0:T(8,128)(2,1)} %concatenate.3, s32[1024]{0:T(1024)S(1)} %pad_clamp_fusion), kind=kCustom, calls=%fused_computation | custom fusion | bytes 16777280 | tf_op jit(solution)/shard_map/gather | solution.py:33
  20.3 5.7 %all-to-all-start = ((bf16[4,1,4,128,2048]{4,3,2,1,0:T(8,128)(2,1)}), bf16[4,1,4,128,2048]{4,3,2,1,0:T(8,128)(2,1)}, u32[]{:S(2)}, u32[]{:S(2)}) async-start(bf16[4,1,4,128,2048]{4,3,2,1,0:T(8,128)(2,1)} %bitcast.58), calls=%async_computation | async-start | bytes 16777216 | tf_op jit(solution)/shard_map/all_to_all | solution.py:34
  25.9 0.0 all-gather.5.cloned.1.call-start
  26.0 0.7 all-gather.5.cloned.1.call-update
  26.7 0.0 all-reduce.4.cloned.1.call-start
  26.7 46.2 %all-gather.7.cloned.1.call-done = bf16[1,2048,768]{2,1,0:T(8,128)(2,1)} async-done(((bf16[1,256,768]{2,1,0:T(8,128)(2,1)}), bf16[1,2048,768]{2,1,0:T(8,128)(2,1)}) %all-gather.7.cloned.1.call-update) | async-done | bytes 3145744 | tf_op jit(solution)/shard_map/all_gather | solution.py:45
  72.9 46.9 %all-to-all-done = bf16[4,1,4,128,2048]{4,3,2,1,0:T(8,128)(2,1)} async-done(((bf16[4,1,4,128,2048]{4,3,2,1,0:T(8,128)(2,1)}), bf16[4,1,4,128,2048]{4,3,2,1,0:T(8,128)(2,1)}, u32[]{:S(2)}, u32[]{:S(2)}) %all-to-all-start) | async-done | bytes 8388640 | tf_op jit(solution)/shard_map/all_to_all | solution.py:34
  119.8 11.7 %fusion.7 = f32[2048,768]{1,0:T(8,128)} fusion(bf16[2048,2048]{1,0:T(8,128)(2,1)} %bitcast.5, bf16[1,2048,768]{2,1,0:T(8,128)(2,1)} %all-gather.7.cloned.1.call-done), kind=kOutput, calls=%fused_computation.8 | convolution fusion | flops 6442450944 | bytes 17825792 | tf_op jit(solution)/shard_map/dot_general | solution.py:43
  131.5 2.3 all-gather.5.cloned.1.call-done
  133.8 10.3 %fusion.9 = f32[2048,768]{1,0:T(8,128)S(1)} fusion(bf16[2048,2048]{1,0:T(8,128)(2,1)} %bitcast.5, bf16[1,2048,768]{2,1,0:T(8,128)(2,1)} %all-gather.5.cloned.1.call-done), kind=kOutput, calls=%fused_computation.10 | convolution fusion | flops 6442450944 | bytes 17825792 | tf_op jit(solution)/shard_map/dot_general | solution.py:38
  144.2 0.0 copy-done.4
  144.2 20.1 %fusion.13 = f32[768,768]{0,1:T(8,128)} fusion(f32[2048,768]{1,0:T(8,128)S(1)} %copy-done.4, f32[2048,768]{1,0:T(8,128)S(1)} %fusion.9), kind=kOutput, calls=%fused_computation.19 | convolution fusion | flops 14503968768 | bytes 14942208 | tf_op jit(solution)/shard_map/dot_general | solution.py:49
  164.2 0.0 all-reduce.4.cloned.1.call-update
  164.2 107.7 %all-reduce.4.cloned.1.call-done = f32[768,768]{0,1:T(8,128)} async-done(((f32[768,768]{0,1:T(8,128)}), f32[768,768]{0,1:T(8,128)}) %all-reduce.4.cloned.1.call-update) | async-done | bytes 2359312 | tf_op jit(solution)/shard_map/psum | solution.py:50
  272.0 3.3 select_add_fusion
  275.2 3.2 copy.24
  278.4 0.0 copy-done.1
  278.4 2.0 fusion.12
  280.4 1.4 copy-done.2
  281.8 11.7 %cholesky.164 = f32[128,128]{1,0:T(8,128)S(1)} custom-call(f32[128,128]{1,0:T(8,128)S(1)} %cholesky.421), custom_call_target="Cholesky" | custom-call | tf_op jit(solution)/shard_map/jit(cholesky)/cholesky | solution.py:51
  293.6 0.1 copy.25
  293.7 9.8 %custom-call.43 = f32[1,128,128]{1,2,0:T(8,128)S(1)} custom-call(f32[1,128,128]{2,1,0:T(8,128)S(1)} %get-tuple-element.13), custom_call_target="InvertDiagBlocksLowerTriangular" | custom-call | tf_op jit(solution)/shard_map/jit(cholesky)/cholesky | solution.py:51
  303.5 0.2 cholesky.338
  303.6 1.5 constant_dynamic-update-slice_fusion.4
  305.1 1.7 convolution_subtract_fusion
  306.8 11.7 %cholesky.187 = f32[128,128]{1,0:T(8,128)S(1)} custom-call(f32[128,128]{1,0:T(8,128)S(1)} %cholesky.425), custom_call_target="Cholesky" | custom-call | tf_op jit(solution)/shard_map/jit(cholesky)/cholesky | solution.py:51
  318.5 0.1 copy.26
  318.6 10.0 %custom-call.44 = f32[1,128,128]{1,2,0:T(8,128)S(1)} custom-call(f32[1,128,128]{2,1,0:T(8,128)S(1)} %get-tuple-element.11), custom_call_target="InvertDiagBlocksLowerTriangular" | custom-call | tf_op jit(solution)/shard_map/jit(cholesky)/cholesky | solution.py:51
  328.6 0.4 convolution_dynamic-update-slice_fusion
  329.0 1.9 convolution_subtract_fusion.1
  331.0 11.7 %cholesky.352 = f32[128,128]{1,0:T(8,128)S(1)} custom-call(f32[128,128]{1,0:T(8,128)S(1)} %cholesky.430), custom_call_target="Cholesky" | custom-call | tf_op jit(solution)/shard_map/jit(cholesky)/cholesky | solution.py:51
  342.8 0.1 copy.27
  342.9 9.8 %custom-call.45 = f32[1,128,128]{1,2,0:T(8,128)S(1)} custom-call(f32[1,128,128]{2,1,0:T(8,128)S(1)} %get-tuple-element.9), custom_call_target="InvertDiagBlocksLowerTriangular" | custom-call | tf_op jit(solution)/shard_map/jit(cholesky)/cholesky | solution.py:51
  352.7 0.4 convolution_dynamic-update-slice_fusion.1
  353.1 2.1 convolution_subtract_fusion.2
  355.2 11.9 %cholesky.371 = f32[128,128]{1,0:T(8,128)S(1)} custom-call(f32[128,128]{1,0:T(8,128)S(1)} %cholesky.435), custom_call_target="Cholesky" | custom-call | tf_op jit(solution)/shard_map/jit(cholesky)/cholesky | solution.py:51
  367.1 0.1 copy.28
  367.2 9.8 %custom-call.46 = f32[1,128,128]{1,2,0:T(8,128)S(1)} custom-call(f32[1,128,128]{2,1,0:T(8,128)S(1)} %get-tuple-element.7), custom_call_target="InvertDiagBlocksLowerTriangular" | custom-call | tf_op jit(solution)/shard_map/jit(cholesky)/cholesky | solution.py:51
  377.1 0.3 convolution_dynamic-update-slice_fusion.2
  377.4 1.9 convolution_subtract_fusion.3
  379.3 11.7 %cholesky.390 = f32[128,128]{1,0:T(8,128)S(1)} custom-call(f32[128,128]{1,0:T(8,128)S(1)} %cholesky.440), custom_call_target="Cholesky" | custom-call | tf_op jit(solution)/shard_map/jit(cholesky)/cholesky | solution.py:51
  391.1 0.1 copy.29
  391.2 9.8 %custom-call.47 = f32[1,128,128]{1,2,0:T(8,128)S(1)} custom-call(f32[1,128,128]{2,1,0:T(8,128)S(1)} %get-tuple-element.5), custom_call_target="InvertDiagBlocksLowerTriangular" | custom-call | tf_op jit(solution)/shard_map/jit(cholesky)/cholesky | solution.py:51
  401.0 0.3 convolution_dynamic-update-slice_fusion.3
  401.3 1.8 convolution_subtract_fusion.4
  403.1 11.7 %cholesky.408 = f32[128,128]{1,0:T(8,128)S(1)} custom-call(f32[128,128]{1,0:T(8,128)S(1)} %convolution_subtract_fusion.4), custom_call_target="Cholesky" | custom-call | tf_op jit(solution)/shard_map/jit(cholesky)/cholesky | solution.py:51
  414.8 0.1 copy.30
  414.9 0.6 compare_reduce_fusion.4
  415.6 0.6 compare_reduce_fusion.5
  416.2 0.7 compare_reduce_fusion.3
  416.9 0.6 compare_reduce_fusion.2
  417.5 0.7 compare_reduce_fusion.1
  418.2 0.7 compare_reduce_fusion
  422.7 0.2 select_select_fusion
  422.9 2.1 convolution_bitcast_fusion
  425.0 0.7 dynamic-slice_bitcast_fusion
  (23 shorter events, 0.3 us)
Async XLA Ops:
  7.2 415.7 %copy-start = (bf16[1,768,256]{2,1,0:T(8,128)(2,1)S(1)}, bf16[1,768,256]{2,1,0:T(8,128)(2,1)}, u32[]{:S(2)}) copy-start(bf16[1,768,256]{2,1,0:T(8,128)(2,1)} %param.9) | copy-start | bytes 1179652
  7.2 65.8 %all-gather.7.cloned.1.call-start = ((), (), s32[]{:S(2)}) async-start(), calls=%async_computation.3 | async-start | bytes 3538944 | tf_op jit(solution)/shard_map/all_gather | solution.py:45
  7.9 5.0 %copy-start.3 = (s32[8,1]{0,1:T(1,128)S(1)}, s32[8,1]{0,1:T(1,128)}, u32[]{:S(2)}) copy-start(s32[8,1]{0,1:T(1,128)} %param.6) | copy-start | bytes 100
  20.3 99.5 %all-to-all-start = ((bf16[4,1,4,128,2048]{4,3,2,1,0:T(8,128)(2,1)}), bf16[4,1,4,128,2048]{4,3,2,1,0:T(8,128)(2,1)}, u32[]{:S(2)}, u32[]{:S(2)}) async-start(bf16[4,1,4,128,2048]{4,3,2,1,0:T(8,128)(2,1)} %bitcast.58), calls=%async_computation | async-start | bytes 16777216 | tf_op jit(solution)/shard_map/all_to_all | solution.py:34
  25.9 107.9 %all-gather.5.cloned.1.call-start = ((), (), s32[]{:S(2)}) async-start(), calls=%async_computation.2 | async-start | bytes 3538944 | tf_op jit(solution)/shard_map/all_gather | solution.py:40
  26.7 245.3 %all-reduce.4.cloned.1.call-start = ((), (), s32[]{:S(2)}) async-start(), calls=%async_computation.1 | async-start | bytes 4718592 | tf_op jit(solution)/shard_map/psum | solution.py:50
  133.8 10.3 %copy-start.4 = (f32[2048,768]{1,0:T(8,128)S(1)}, f32[2048,768]{1,0:T(8,128)}, u32[]{:S(2)}) copy-start(f32[2048,768]{1,0:T(8,128)} %fusion.7) | copy-start | bytes 18874372
  275.2 3.2 copy-start.1
  280.4 1.4 copy-start.2
Sparse Core Ops, SparseCore 0:
  10.2 62.7 all-gather.6
  75.1 58.6 all-gather.4
  164.4 107.5 all-reduce.3
where the time goes:
time: 438 us; the launch traced here: 433 us
  waiting for transfers between devices  204 us (47%)
  other arithmetic  130 us (30%)
  matrix products  56.5 us (13%)
  between operations  18.3 us (4%)
  local copies, waits for them, and re-layouts  18.2 us (4%)
  starting transfers between devices  5.77 us (1%)
    another operation x23, other arithmetic, on_device(): upper = jnp.linalg.cholesky(total).T  124 us
    psum x1, waiting for transfers between devices, on_device(): total = lax.psum(gram, 'dp') + damping * eye  108 us
    all_to_all x1, waiting for transfers between devices, on_device(): lax.all_to_all(outgoing, 'expert', split_axis=0, concat_axis=0, tiled=True)  46.9 us
    all_gather x1, waiting for transfers between devices, on_device(): lax.all_gather(up_weight[0], 'dp', axis=0, tiled=True)  46.2 us
    dot_general x1, matrix products, on_device(): jnp.dot(hidden.T, hidden, precision=lax.Precision.HIGHEST) / float(rows_avg)  20.1 us
    another operation x10, matrix products, on_device(): upper = jnp.linalg.cholesky(total).T  12.3 us
    dot_general x1, matrix products, on_device(): jnp.dot(rows, lax.all_gather(up_weight[0], 'dp', axis=0, tiled=True), pre...  11.7 us
    dot_general x1, matrix products, on_device(): jnp.dot(rows, lax.all_gather(gate_weight[0], 'dp', axis=0, tiled=True), p...  10.3 us
  transfers between devices with their start and end apart: 4, of which 4 were waited for; matrix products, arithmetic and copies ran while one was open for 6% of the time, Pallas kernels for 0%

commit v1 on v0

--- a/solution.py
+++ b/solution.py
@@ -47,7 +47,7 @@
     )
     hidden = jax.nn.silu(gate) * lifted
     gram = jnp.dot(hidden.T, hidden, precision=lax.Precision.HIGHEST) / float(rows_avg)
-    total = lax.psum(gram, "dp") + damping * eye
+    total = jnp.sum(lax.all_gather(gram, "dp"), axis=0) + damping * eye
     upper = jnp.linalg.cholesky(total).T
     factors = [lax.dynamic_slice_in_dim(upper, lax.axis_index("dp") * my_rows, my_rows, 0)]
     products = [jnp.dot(upper, down_weight[0].astype(jnp.float32), precision=lax.Precision.HIGHEST)]

time: 438 us -> 696 us (1.59)
  waiting for transfers between devices: 204 us -> 458 us
    all_gather x0 -> x1, waiting for transfers between devices: none -> 361 us  [on_device(): total = jnp.sum(lax.all_gather(gram, 'dp'), axis=0) + damping * eye]
    psum x1 -> x0, waiting for transfers between devices: 108 us -> none  [on_device(): total = lax.psum(gram, 'dp') + damping * eye]
    reduce_sum x0 -> x1, other arithmetic: none -> 7.87 us  [on_device(): total = jnp.sum(lax.all_gather(gram, 'dp'), axis=0) + damping * eye]
  transfers between devices with their start and end apart: 4 -> 4, of which waited for: 4 -> 4; matrix products, arithmetic and copies ran while one was open for 6% -> 3% of each run, Pallas kernels for 0% -> 0%
where the time goes in v1:
time: 696 us; the launch traced here: 690 us
  waiting for transfers between devices  458 us (66%)
  other arithmetic  135 us (19%)
  matrix products  54.7 us (8%)
  local copies, waits for them, and re-layouts  18.7 us (3%)
  between operations  18 us (3%)
    all_gather x1, waiting for transfers between devices, on_device(): total = jnp.sum(lax.all_gather(gram, 'dp'), axis=0) + damping * eye  361 us
    another operation x23, other arithmetic, on_device(): upper = jnp.linalg.cholesky(total).T  124 us
    all_to_all x1, waiting for transfers between devices, on_device(): lax.all_to_all(outgoing, 'expert', split_axis=0, concat_axis=0, tiled=True)  46.9 us
    all_gather x1, waiting for transfers between devices, on_device(): lax.all_gather(up_weight[0], 'dp', axis=0, tiled=True)  46.2 us
    dot_general x1, matrix products, on_device(): jnp.dot(hidden.T, hidden, precision=lax.Precision.HIGHEST) / float(rows_avg)  19.4 us
  transfers between devices with their start and end apart: 4, of which 4 were waited for; matrix products, arithmetic and copies ran while one was open for 3% of the time, Pallas kernels for 0%

profile of v1, /device:TPU:0, one launch (start us, length us, event | category | flops | bytes accessed | tf_op | source)
XLA Modules:
  0.0 689.9 jit_solution(8153738156929625589)
XLA Ops:
  7.2 0.0 copy-start
  7.2 0.0 all-gather.9.cloned.1.call-start
  7.2 0.7 all-gather.9.cloned.1.call-update
  7.9 0.0 copy-start.2
  7.9 5.0 concatenate.3
  12.9 0.0 copy-done.2
  12.9 0.2 convert_reduce_fusion.1
  13.1 0.1 convert_reduce_fusion
  13.2 7.1 %gather_fusion = bf16[16,128,2048]{2,1,0:T(8,128)(2,1)} fusion(bf16[9,128,2048]{2,1,0:T(8,128)(2,1)} %concatenate.3, s32[1024]{0:T(1024)S(1)} %pad_clamp_fusion), kind=kCustom, calls=%fused_computation | custom fusion | bytes 16777280 | tf_op jit(solution)/shard_map/gather | solution.py:33
  20.3 5.7 all-to-all-start
  25.9 0.0 all-gather.7.cloned.1.call-start
  26.0 0.7 all-gather.7.cloned.1.call-update
  26.7 0.0 all-gather.11.cloned.1.call-start
  26.7 46.2 %all-gather.9.cloned.1.call-done = bf16[1,2048,768]{2,1,0:T(8,128)(2,1)} async-done(((bf16[1,256,768]{2,1,0:T(8,128)(2,1)}), bf16[1,2048,768]{2,1,0:T(8,128)(2,1)}) %all-gather.9.cloned.1.call-update) | async-done | bytes 3145744 | tf_op jit(solution)/shard_map/all_gather | solution.py:45
  72.9 46.9 %all-to-all-done = bf16[4,1,4,128,2048]{4,3,2,1,0:T(8,128)(2,1)} async-done(((bf16[4,1,4,128,2048]{4,3,2,1,0:T(8,128)(2,1)}), bf16[4,1,4,128,2048]{4,3,2,1,0:T(8,128)(2,1)}, u32[]{:S(2)}, u32[]{:S(2)}) %all-to-all-start) | async-done | bytes 8388640 | tf_op jit(solution)/shard_map/all_to_all | solution.py:34
  119.8 11.7 %fusion.7 = f32[2048,768]{1,0:T(8,128)} fusion(bf16[2048,2048]{1,0:T(8,128)(2,1)} %bitcast.5, bf16[1,2048,768]{2,1,0:T(8,128)(2,1)} %all-gather.9.cloned.1.call-done), kind=kOutput, calls=%fused_computation.8 | convolution fusion | flops 6442450944 | bytes 17825792 | tf_op jit(solution)/shard_map/dot_general | solution.py:43
  131.5 2.3 all-gather.7.cloned.1.call-done
  133.8 0.0 copy-start.3
  133.8 10.4 %fusion.9 = f32[2048,768]{1,0:T(8,128)S(1)} fusion(bf16[2048,2048]{1,0:T(8,128)(2,1)} %bitcast.5, bf16[1,2048,768]{2,1,0:T(8,128)(2,1)} %all-gather.7.cloned.1.call-done), kind=kOutput, calls=%fused_computation.10 | convolution fusion | flops 6442450944 | bytes 17825792 | tf_op jit(solution)/shard_map/dot_general | solution.py:38
  144.3 0.0 copy-done.3
  144.3 19.4 %fusion.12 = f32[768,768]{1,0:T(8,128)} fusion(f32[2048,768]{1,0:T(8,128)S(1)} %copy-done.3, f32[2048,768]{1,0:T(8,128)S(1)} %fusion.9), kind=kOutput, calls=%fused_computation.18 | convolution fusion | flops 14503968768 | bytes 14942208 | tf_op jit(solution)/shard_map/dot_general | solution.py:49
  163.7 0.0 all-gather.11.cloned.1.call-update
  163.7 361.5 %all-gather.11.cloned.1.call-done = f32[6144,768]{1,0:T(8,128)} async-done(((f32[768,768]{1,0:T(8,128)}), f32[6144,768]{1,0:T(8,128)}) %all-gather.11.cloned.1.call-update) | async-done | bytes 18874384 | tf_op jit(solution)/shard_map/all_gather | solution.py:50
  525.2 7.9 %reduce_sum.41 = f32[768,768]{1,0:T(8,128)S(1)} reduce(f32[8,768,768]{2,1,0:T(8,128)} %bitcast.56, f32[]{:T(128)} %constant.248.clone.1), dimensions={0}, to_apply=%region_3.4 | reduce | flops 4128768 | bytes 21233668 | tf_op jit(solution)/shard_map/reduce_sum | solution.py:50
  533.1 2.1 copy.21
  535.2 2.0 add_multiply_fusion
  537.2 0.0 copy-start.1
  537.2 1.4 copy-done.1
  538.6 11.7 %cholesky.164 = f32[128,128]{1,0:T(8,128)S(1)} custom-call(f32[128,128]{1,0:T(8,128)S(1)} %cholesky.421), custom_call_target="Cholesky" | custom-call | tf_op jit(solution)/shard_map/jit(cholesky)/cholesky | solution.py:51
  550.4 0.2 cholesky.338
  550.5 9.8 %custom-call.43 = f32[1,128,128]{1,2,0:T(8,128)S(1)} custom-call(f32[1,128,128]{2,1,0:T(8,128)S(1)} %get-tuple-element.25), custom_call_target="InvertDiagBlocksLowerTriangular" | custom-call | tf_op jit(solution)/shard_map/jit(cholesky)/cholesky | solution.py:51
  560.3 1.5 fusion.20
  561.8 0.9 copy.22
  562.7 1.7 convolution_subtract_fusion
  564.4 11.7 %cholesky.187 = f32[128,128]{1,0:T(8,128)S(1)} custom-call(f32[128,128]{1,0:T(8,128)S(1)} %cholesky.425), custom_call_target="Cholesky" | custom-call | tf_op jit(solution)/shard_map/jit(cholesky)/cholesky | solution.py:51
  576.1 1.0 constant_dynamic-update-slice_fusion.4
  577.1 0.6 compare_reduce_fusion.4
  577.8 0.6 compare_reduce_fusion.5
  578.4 10.0 %custom-call.44 = f32[1,128,128]{1,2,0:T(8,128)S(1)} custom-call(f32[1,128,128]{2,1,0:T(8,128)S(1)} %get-tuple-element.22), custom_call_target="InvertDiagBlocksLowerTriangular" | custom-call | tf_op jit(solution)/shard_map/jit(cholesky)/cholesky | solution.py:51
  588.4 0.4 convolution_dynamic-update-slice_fusion
  588.8 1.5 convolution_subtract_fusion.1
  590.3 11.7 %cholesky.352 = f32[128,128]{1,0:T(8,128)S(1)} custom-call(f32[128,128]{1,0:T(8,128)S(1)} %cholesky.430), custom_call_target="Cholesky" | custom-call | tf_op jit(solution)/shard_map/jit(cholesky)/cholesky | solution.py:51
  602.1 0.6 compare_reduce_fusion.3
  602.7 9.8 %custom-call.45 = f32[1,128,128]{1,2,0:T(8,128)S(1)} custom-call(f32[1,128,128]{2,1,0:T(8,128)S(1)} %get-tuple-element.19), custom_call_target="InvertDiagBlocksLowerTriangular" | custom-call | tf_op jit(solution)/shard_map/jit(cholesky)/cholesky | solution.py:51
  612.5 0.3 convolution_dynamic-update-slice_fusion.1
  612.8 1.6 convolution_subtract_fusion.2
  614.4 12.1 %cholesky.371 = f32[128,128]{1,0:T(8,128)S(1)} custom-call(f32[128,128]{1,0:T(8,128)S(1)} %cholesky.435), custom_call_target="Cholesky" | custom-call | tf_op jit(solution)/shard_map/jit(cholesky)/cholesky | solution.py:51
  626.5 0.7 compare_reduce_fusion.2
  627.2 9.8 %custom-call.46 = f32[1,128,128]{1,2,0:T(8,128)S(1)} custom-call(f32[1,128,128]{2,1,0:T(8,128)S(1)} %get-tuple-element.16), custom_call_target="InvertDiagBlocksLowerTriangular" | custom-call | tf_op jit(solution)/shard_map/jit(cholesky)/cholesky | solution.py:51
  637.0 0.3 convolution_dynamic-update-slice_fusion.2
  637.3 1.5 convolution_subtract_fusion.3
  638.8 11.7 %cholesky.390 = f32[128,128]{1,0:T(8,128)S(1)} custom-call(f32[128,128]{1,0:T(8,128)S(1)} %cholesky.440), custom_call_target="Cholesky" | custom-call | tf_op jit(solution)/shard_map/jit(cholesky)/cholesky | solution.py:51
  650.5 0.7 compare_reduce_fusion.1
  651.2 9.8 %custom-call.47 = f32[1,128,128]{1,2,0:T(8,128)S(1)} custom-call(f32[1,128,128]{2,1,0:T(8,128)S(1)} %get-tuple-element.13), custom_call_target="InvertDiagBlocksLowerTriangular" | custom-call | tf_op jit(solution)/shard_map/jit(cholesky)/cholesky | solution.py:51
  661.0 0.2 convolution_dynamic-update-slice_fusion.3
  661.3 1.3 convolution_subtract_fusion.4
  662.6 11.9 %cholesky.408 = f32[128,128]{1,0:T(8,128)S(1)} custom-call(f32[128,128]{1,0:T(8,128)S(1)} %convolution_subtract_fusion.4), custom_call_target="Cholesky" | custom-call | tf_op jit(solution)/shard_map/jit(cholesky)/cholesky | solution.py:51
  674.5 0.7 compare_reduce_fusion
  679.0 0.2 select_select_fusion
  679.2 0.0 copy-done
  679.2 2.9 convolution_bitcast_fusion
  682.2 0.2 dynamic-slice_bitcast_fusion
  682.3 0.9 copy.27
  (14 shorter events, 0.3 us)
Async XLA Ops:
  7.2 672.1 %copy-start = (bf16[1,768,256]{2,1,0:T(8,128)(2,1)S(1)}, bf16[1,768,256]{2,1,0:T(8,128)(2,1)}, u32[]{:S(2)}) copy-start(bf16[1,768,256]{2,1,0:T(8,128)(2,1)} %param.9) | copy-start | bytes 1179652
  7.2 65.8 %all-gather.9.cloned.1.call-start = ((), (), s32[]{:S(2)}) async-start(), calls=%async_computation.2 | async-start | bytes 3538944 | tf_op jit(solution)/shard_map/all_gather | solution.py:45
  7.9 5.0 copy-start.2
  20.3 99.5 %all-to-all-start = ((bf16[4,1,4,128,2048]{4,3,2,1,0:T(8,128)(2,1)}), bf16[4,1,4,128,2048]{4,3,2,1,0:T(8,128)(2,1)}, u32[]{:S(2)}, u32[]{:S(2)}) async-start(bf16[4,1,4,128,2048]{4,3,2,1,0:T(8,128)(2,1)} %bitcast.54), calls=%async_computation | async-start | bytes 16777216 | tf_op jit(solution)/shard_map/all_to_all | solution.py:34
  25.9 107.9 %all-gather.7.cloned.1.call-start = ((), (), s32[]{:S(2)}) async-start(), calls=%async_computation.1 | async-start | bytes 3538944 | tf_op jit(solution)/shard_map/all_gather | solution.py:40
  26.7 498.5 %all-gather.11.cloned.1.call-start = ((), (), s32[]{:S(2)}) async-start(), calls=%async_computation.3 | async-start | bytes 21233664 | tf_op jit(solution)/shard_map/all_gather | solution.py:50
  133.8 10.4 %copy-start.3 = (f32[2048,768]{1,0:T(8,128)S(1)}, f32[2048,768]{1,0:T(8,128)}, u32[]{:S(2)}) copy-start(f32[2048,768]{1,0:T(8,128)} %fusion.7) | copy-start | bytes 18874372
  537.2 1.4 copy-start.1
Sparse Core Ops, SparseCore 0:
  10.2 62.7 all-gather.8
  75.1 58.6 all-gather.6
  163.8 361.3 all-gather.10
